TPU v7x, 32 devices: a whole 2x2x4 slice. The times are simulated.
32 devices in a mesh: row: 8 (over z, x), col: 4 (over y, core).
Axes of the slice: x: 2, y: 2, z: 4, core: 2. Of those that a mesh axis runs over, the one named last changes fastest.
Arguments:
- panel: float32 [2560, 256], P('row', 'col'), may hold values from 0 to 65520, as said below
- trail: float32 [2560, 16384], P('row', 'col'), may hold values from 0 to 65520, as said below
- leaf_pick: int32 [8, 256], P('row'), may hold values from 0 to 319, as said below
- node_pick: int32 [7, 256], replicated, may hold values from 0 to 511, as said below
Outputs:
- schur: float32 [2560, 16384], P('row', 'col')
- multipliers: float32 [2560, 256], P('row')
Inputs may be any that keep to these rules, and one draw needn't show every extreme that they name: `leaf_pick`: each row holds 256 different local row numbers. `node_pick`: each row holds 256 different positions among the node's 2 * 256 candidates. Entries are whole residues; the panel rows of pivot_ids, in that order, form a unit upper-triangular matrix modulo 65521. `trail`: entries are whole residues.
All inputs are finite; a program needn't handle non-finite values.
Results may differ from a plain program's by a relative error of at most 0.0003.
Values sent between devices are 32-bit elements; how exact they have to be, the bound alone decides.
No kernel may reach another device: no remote copies, remote signals or barrier semaphores. Data moves between devices by JAX's collectives and lax.ppermute only.
A program may use at most 128 MiB of HBM per device.

v0:
```python
import jax
import jax.numpy as jnp
from jax import lax
from jax.sharding import PartitionSpec as P

MODULUS = 65521.0


def swapped(block, axis, bit):
    count = lax.axis_size(axis)
    route = []
    for low in range(count):
        high = low | 1 << bit
        if high != low and high < count:
            route += [(low, high), (high, low)]
    return lax.ppermute(block, axis, route)


def residue(values):
    return jnp.mod(values, MODULUS)


def limbs(values):
    upper_limb = jnp.floor(values / 256.0)
    lower_limb = values - 256.0 * upper_limb
    return (upper_limb.astype(jnp.bfloat16), lower_limb.astype(jnp.bfloat16))


def modmul(first_factor, second_factor):
    first_upper, first_lower = limbs(first_factor)
    second_upper, second_lower = limbs(second_factor)
    high_part = residue(jnp.dot(first_upper, second_upper, preferred_element_type=jnp.float32))
    cross_one = residue(jnp.dot(first_upper, second_lower, preferred_element_type=jnp.float32))
    cross_two = residue(jnp.dot(first_lower, second_upper, preferred_element_type=jnp.float32))
    low_part = residue(jnp.dot(first_lower, second_lower, preferred_element_type=jnp.float32))
    middle = residue(cross_one + cross_two)
    return residue(residue(15.0 * high_part) + residue(256.0 * middle) + low_part)


def invert_unit(pivot_block):
    width = pivot_block.shape[0]
    identity = jnp.eye(width, dtype=jnp.float32)
    nilpotent = pivot_block - identity
    inverse = residue(identity - nilpotent + MODULUS)
    power = nilpotent
    for section in range((width - 1).bit_length() - 1):
        power = modmul(power, power)
        inverse = modmul(inverse, residue(identity + power))
    return inverse


def merge_candidates(owned, partner, place, height, devices, node_pick):
    upper_half = place >> height & 1
    node_index = devices - (devices >> height) + (place >> height + 1)
    picked = node_pick[node_index]

    def join(mine_part, their_part):
        lower_first = jnp.concatenate([mine_part, their_part], axis=0)
        upper_first = jnp.concatenate([their_part, mine_part], axis=0)
        stacked = jnp.where(upper_half == 0, lower_first, upper_first)
        return stacked[picked]

    return jax.tree.map(join, owned, partner)


def per_device(panel, trail, leaf_pick, node_pick):
    row_count = panel.shape[0]
    part_width = panel.shape[1]
    place = lax.axis_index("row")
    devices = lax.axis_size("row")
    depth_count = devices.bit_length() - 1
    own_picks = leaf_pick[0]
    held = (panel[own_picks], place * row_count + own_picks)
    for height in range(depth_count):
        partner = swapped((held[0], held[1]), "row", height)
        held = merge_candidates(held, partner, place, height, devices, node_pick)
    block_part, row_ids = held
    owned = (row_ids // row_count == place).astype(jnp.float32)[:, None]
    local_rows = row_ids % row_count
    pivot_trail = lax.psum(trail[local_rows] * owned, "row")
    pivot_block = lax.all_gather(block_part, "col", axis=1, tiled=True)
    inverse = invert_unit(pivot_block)
    first_col = lax.axis_index("col") * part_width
    inverse_rows = lax.dynamic_slice_in_dim(inverse, first_col, part_width, 0)
    factors = residue(lax.psum(modmul(panel, inverse_rows), "col"))
    remainder = residue(trail + (MODULUS - modmul(factors, pivot_trail)))
    return (remainder / MODULUS, factors / MODULUS)


def solution(mesh):
    in_specs = (P("row", "col"), P("row", "col"), P("row", None), P())
    out_specs = (P("row", "col"), P("row", None))
    return jax.shard_map(
        per_device, mesh=mesh, in_specs=in_specs, out_specs=out_specs, check_vma=False
    )
```

profile of v0, /device:TPU:0, one launch (start us, length us, event | category | flops | bytes accessed | tf_op | source)
XLA Modules:
  0.0 318.1 jit_solution(15602679436969307907)
XLA Ops:
  7.2 1.0 copy.8
  9.6 3.0 collective-permute-start
  14.2 2.7 collective-permute-done.3
  16.9 1.9 gather_fusion.4
  18.9 1.6 collective-permute-start.4
  20.5 2.0 collective-permute-done.4
  22.5 1.9 gather_fusion.5
  24.5 2.7 collective-permute-start.5
  27.1 1.9 collective-permute-done.5
  29.0 1.9 gather_fusion.6
  31.8 1.6 collective-permute-start.1
  33.4 4.7 %collective-permute-done.1 = f32[256,64]{1,0:T(8,128)S(1)} collective-permute-done((f32[256,64]{1,0:T(8,128)S(1)}, f32[256,64]{1,0:T(8,128)S(1)}, u32[]{:S(2)}, u32[]{:S(2)}) %collective-permute-start.1) | collective-permute-done | bytes 65568 | tf_op jit(solution)/shard_map/ppermute | solution.py:16
  38.9 2.7 collective-permute-start.2
  41.6 8.2 %gather_fusion.7 = f32[256,4096]{1,0:T(8,128)} fusion(f32[320,4096]{1,0:T(8,128)} %param.5, s32[1024]{0:T(1024)S(1)} %pad_clamp_fusion), kind=kCustom, calls=%fused_computation.7 | custom fusion | bytes 8389632 | tf_op jit(solution)/shard_map/gather | solution.py:80
  50.7 6.0 %all-gather = f32[256,256]{0,1:T(8,128)S(1)} all-gather(f32[256,64]{0,1:T(8,128)S(1)} %copy.9), channel_id=2, replica_groups=mesh['row'=8,'col'=4] {'col'}, dimensions={1}, use_global_device_ids=true | all-gather | bytes 327680 | tf_op jit(solution)/shard_map/all_gather | solution.py:81
  60.7 1.2 add_select_fusion.118
  64.8 1.1 add_select_fusion.101
  68.8 1.1 add_select_fusion.84
  69.9 1.1 add_select_fusion.76
  73.0 1.1 add_select_fusion.67
  76.9 1.1 add_select_fusion.50
  80.9 1.1 add_select_fusion.33
  82.0 1.1 add_select_fusion.24
  86.1 1.9 add_select_fusion.10
  88.0 4.8 %broadcast_multiply_fusion = f32[256,4096]{1,0:T(8,128)} fusion(f32[256,4096]{1,0:T(8,128)} %gather_fusion.7, f32[256]{0:T(256)S(1)} %compare_convert_fusion), kind=kLoop, calls=%fused_computation.37 | loop fusion | flops 1048576 | bytes 8389632 | tf_op jit(solution)/shard_map/mul | solution.py:80
  92.8 25.4 %all-reduce.3.cloned.1.call-done = f32[320,256]{1,0:T(8,128)} async-done(((f32[320,256]{1,0:T(8,128)}), f32[320,256]{1,0:T(8,128)}) %all-reduce.3.cloned.1.call-update) | async-done | bytes 327696 | tf_op jit(solution)/shard_map/psum | solution.py:85
  118.3 1.9 broadcast_multiply_fusion.1
  120.1 158.8 %all-reduce.5.cloned.1.call-done = f32[256,4096]{1,0:T(8,128)} async-done(((f32[256,4096]{1,0:T(8,128)}), f32[256,4096]{1,0:T(8,128)}) %all-reduce.5.cloned.1.call-update) | async-done | bytes 4194320 | tf_op jit(solution)/shard_map/psum | solution.py:80
  279.0 4.5 %convolution_remainder_fusion.3 = f32[320,4096]{1,0:T(8,128)S(1)} fusion(f32[256,4096]{1,0:T(8,128)} %all-reduce.5.cloned.1.call-done, f32[320,256]{1,0:T(8,128)} %all-reduce.3.cloned.1.call-done), kind=kOutput, calls=%fused_computation.20 | convolution fusion | flops 676282368 | bytes 9764864 | tf_op jit(solution)/shard_map/dot_general | solution.py:32
  283.5 2.8 convolution_remainder_fusion.2
  286.3 2.6 convolution_remainder_fusion.1
  288.9 22.2 %fusion.12 = f32[320,4096]{1,0:T(8,128)} fusion(f32[320,4096]{1,0:T(8,128)S(1)} %bitcast.22, f32[320,4096]{1,0:T(8,128)S(1)} %convolution_remainder_fusion.1, f32[320,4096]{1,0:T(8,128)S(1)} %convolution_remainder_fusion.2, f32[320,4096]{1,0:T(8,128)S(1)} %convolution_remainder_fusion.3, f32[256,4096]{1,0:T(8,128)S(1)} %copy-done, f32[320,256]{1,0:T(8,128)S(1)} %copy-done.1), kind=kOutput, calls=%fused_computation.33 | convolution fusion | flops 754565120 | bytes 30736384 | tf_op jit(solution)/shard_map/dot_general | solution.py:35
  (94 shorter events, 25.9 us)
Async XLA Ops:
  7.2 111.1 %all-reduce.3.cloned.1.call-start = ((), (), s32[]{:S(2)}) async-start(), calls=%async_computation | async-start | bytes 655360 | tf_op jit(solution)/shard_map/psum | solution.py:85
  9.6 21.4 %collective-permute-start = (f32[256,64]{1,0:T(8,128)S(1)}, f32[256,64]{1,0:T(8,128)S(1)}, u32[]{:S(2)}, u32[]{:S(2)}) collective-permute-start(f32[256,64]{1,0:T(8,128)S(1)} %gather_fusion), channel_id=1, source_target_pairs={{0,4},{4,0},{8,12},{12,8},{16,20},{20,16},{24,28},{28,24},{1,5},{5... | collective-permute-start | bytes 196616 | tf_op jit(solution)/shard_map/ppermute | solution.py:16
  13.3 3.6 %collective-permute-start.3 = (s32[256]{0:T(256)S(1)}, s32[256]{0:T(256)S(1)}, u32[]{:S(2)}, u32[]{:S(2)}) collective-permute-start(s32[256]{0:T(256)S(1)} %bitcast.29), channel_id=1, source_target_pairs={{0,4},{4,0},{8,12},{12,8},{16,20},{20,16},{24,28},{28,24},{1,5},{5... | collective-permute-start | bytes 3080 | tf_op jit(solution)/shard_map/ppermute | solution.py:16
  18.9 3.6 %collective-permute-start.4 = (s32[256]{0:T(256)S(1)}, s32[256]{0:T(256)S(1)}, u32[]{:S(2)}, u32[]{:S(2)}) collective-permute-start(s32[256]{0:T(256)S(1)} %gather_fusion.4), channel_id=1, source_target_pairs={{0,8},{8,0},{4,12},{12,4},{16,24},{24,16},{20,28},{28,20},{1,9},{9... | collective-permute-start | bytes 3080 | tf_op jit(solution)/shard_map/ppermute | solution.py:16
  24.5 4.5 %collective-permute-start.5 = (s32[256]{0:T(256)S(1)}, s32[256]{0:T(256)S(1)}, u32[]{:S(2)}, u32[]{:S(2)}) collective-permute-start(s32[256]{0:T(256)S(1)} %gather_fusion.5), channel_id=1, source_target_pairs={{0,16},{16,0},{4,20},{20,4},{8,24},{24,8},{12,28},{28,12},{1,17},{... | collective-permute-start | bytes 3080 | tf_op jit(solution)/shard_map/ppermute | solution.py:16
  31.8 6.3 %collective-permute-start.1 = (f32[256,64]{1,0:T(8,128)S(1)}, f32[256,64]{1,0:T(8,128)S(1)}, u32[]{:S(2)}, u32[]{:S(2)}) collective-permute-start(f32[256,64]{1,0:T(8,128)S(1)} %gather_fusion.1), channel_id=1, source_target_pairs={{0,8},{8,0},{4,12},{12,4},{16,24},{24,16},{20,28},{28,20},{1,9},{9... | collective-permute-start | bytes 196616 | tf_op jit(solution)/shard_map/ppermute | solution.py:16
  38.9 10.9 %collective-permute-start.2 = (f32[256,64]{1,0:T(8,128)S(1)}, f32[256,64]{1,0:T(8,128)S(1)}, u32[]{:S(2)}, u32[]{:S(2)}) collective-permute-start(f32[256,64]{1,0:T(8,128)S(1)} %gather_fusion.2), channel_id=1, source_target_pairs={{0,16},{16,0},{4,20},{20,4},{8,24},{24,8},{12,28},{28,12},{1,17},{... | collective-permute-start | bytes 196616 | tf_op jit(solution)/shard_map/ppermute | solution.py:16
  82.0 3.2 copy-start.2
  88.0 191.0 %all-reduce.5.cloned.1.call-start = ((), (), s32[]{:S(2)}) async-start(), calls=%async_computation.1 | async-start | bytes 8388608 | tf_op jit(solution)/shard_map/psum | solution.py:80
  120.1 163.3 %copy-start.1 = (f32[320,256]{1,0:T(8,128)S(1)}, f32[320,256]{1,0:T(8,128)}, u32[]{:S(2)}) copy-start(f32[320,256]{1,0:T(8,128)} %all-reduce.3.cloned.1.call-done) | copy-start | bytes 983044
  279.0 4.5 %copy-start = (f32[256,4096]{1,0:T(8,128)S(1)}, f32[256,4096]{1,0:T(8,128)}, u32[]{:S(2)}) copy-start(f32[256,4096]{1,0:T(8,128)} %all-reduce.5.cloned.1.call-done) | copy-start | bytes 12582916
  283.5 5.4 %slice-start = ((s8[5242880]{0:T(1024)(128)(4,1)}), s8[4194304]{0:T(1024)(128)(4,1)S(1)}, s32[]{:S(2)}) async-start(s8[5242880]{0:T(1024)(128)(4,1)} %bitcast.21), calls=%async_computation.2 | async-start | bytes 8388608
  286.3 2.6 slice-start.1
Sparse Core Ops, SparseCore 0:
  88.1 30.1 all-reduce.2
  122.5 156.3 all-reduce.4
where the time goes:
time: 323 us; the launch traced here: 318 us
  waiting for transfers between devices  196 us (61%)
  matrix products  62.6 us (19%)
  local copies, waits for them, and re-layouts  18.2 us (6%)
  between operations  14.8 us (5%)
  starting transfers between devices  11.8 us (4%)
  other arithmetic  9.13 us (3%)
  blocking collectives  5.95 us (2%)
    psum x1, waiting for transfers between devices, per_device(): pivot_trail = lax.psum(trail[local_rows] * owned, 'row')  159 us
    dot_general x16, matrix products, modmul(): jnp.dot(first_lower, second_lower, preferred_element_type=jnp.float32)  37.5 us
    psum x1, waiting for transfers between devices, per_device(): factors = residue(lax.psum(modmul(panel, inverse_rows), 'col'))  25.4 us
    ppermute x6, starting transfers between devices, swapped(): return lax.ppermute(block, axis, route)  11.7 us
    ppermute x6, waiting for transfers between devices, swapped(): return lax.ppermute(block, axis, route)  11.3 us
    dot_general x16, matrix products, modmul(): jnp.dot(first_upper, second_upper, preferred_element_type=jnp.float32)  9.38 us
    gather x1, local copies, waits for them, and re-layouts, per_device(): pivot_trail = lax.psum(trail[local_rows] * owned, 'row')  8.18 us
    gather x7, local copies, waits for them, and re-layouts, join(): return stacked[picked]  8.1 us
  transfers between devices with their start and end apart: 8, of which 6 were waited for; matrix products, arithmetic and copies ran while one was open for 7% of the time, Pallas kernels for 0%

commit v1 on v0

--- a/solution.py
+++ b/solution.py
@@ -77,7 +77,9 @@
     block_part, row_ids = held
     owned = (row_ids // row_count == place).astype(jnp.float32)[:, None]
     local_rows = row_ids % row_count
-    pivot_trail = lax.psum(trail[local_rows] * owned, "row")
+    q_in = trail[local_rows] * owned
+    now = lax.all_gather(q_in, "row")
+    pivot_trail = jnp.sum(now, 0)
     pivot_block = lax.all_gather(block_part, "col", axis=1, tiled=True)
     inverse = invert_unit(pivot_block)
     first_col = lax.axis_index("col") * part_width

time: 323 us -> 786 us (2.43)
  waiting for transfers between devices: 196 us -> 640 us
  other arithmetic: 9.13 us -> 23.6 us
    all_gather x0 -> x1, waiting for transfers between devices: none -> 608 us  [per_device(): now = lax.all_gather(q_in, 'row')]
    psum x1 -> x0, waiting for transfers between devices: 159 us -> none  [per_device(): pivot_trail = lax.psum(trail[local_rows] * owned, 'row')]
    reduce_sum x0 -> x1, other arithmetic: none -> 14 us  [per_device(): pivot_trail = jnp.sum(now, 0)]
  transfers between devices with their start and end apart: 8 -> 8, of which waited for: 6 -> 5; matrix products, arithmetic and copies ran while one was open for 7% -> 3% of each run, Pallas kernels for 0% -> 0%
where the time goes in v1:
time: 786 us; the launch traced here: 781 us
  waiting for transfers between devices  640 us (81%)
  matrix products  62.2 us (8%)
  other arithmetic  23.6 us (3%)
  local copies, waits for them, and re-layouts  18.2 us (2%)
  between operations  16.3 us (2%)
  starting transfers between devices  14.2 us (2%)
    all_gather x1, waiting for transfers between devices, per_device(): now = lax.all_gather(q_in, 'row')  608 us
    dot_general x16, matrix products, modmul(): jnp.dot(first_lower, second_lower, preferred_element_type=jnp.float32)  37.3 us
    psum x1, waiting for transfers between devices, per_device(): factors = residue(lax.psum(modmul(panel, inverse_rows), 'col'))  26.2 us
  transfers between devices with their start and end apart: 8, of which 5 were waited for; matrix products, arithmetic and copies ran while one was open for 3% of the time, Pallas kernels for 0%

profile of v1, /device:TPU:0, one launch (start us, length us, event | category | flops | bytes accessed | tf_op | source)
XLA Modules:
  0.0 780.8 jit_solution(15529044774534345553)
XLA Ops:
  8.7 3.0 collective-permute-start.3
  12.4 1.0 copy.8
  15.1 1.9 gather_fusion.4
  17.0 2.1 collective-permute-start.4
  19.2 1.5 collective-permute-done.4
  20.7 1.9 gather_fusion.5
  22.7 3.1 collective-permute-start.5
  25.8 1.5 collective-permute-done.5
  27.4 1.9 gather_fusion.6
  30.1 2.0 collective-permute-start.1
  32.1 3.0 collective-permute-done.1
  35.9 3.8 collective-permute-start.2
  39.8 8.2 %gather_fusion.7 = f32[256,4096]{1,0:T(8,128)} fusion(f32[320,4096]{1,0:T(8,128)} %param.5, s32[1024]{0:T(1024)S(1)} %pad_clamp_fusion), kind=kCustom, calls=%fused_computation.7 | custom fusion | bytes 8389632 | tf_op jit(solution)/shard_map/gather | solution.py:80
  48.8 6.0 all-gather
  55.7 0.9 add_select_fusion.127
  67.3 1.2 add_select_fusion.118
  69.9 1.1 add_select_fusion.101
  72.2 1.1 add_select_fusion.84
  74.5 1.1 add_select_fusion.67
  76.8 1.1 add_select_fusion.50
  79.0 1.1 add_select_fusion.24
  80.1 1.1 add_select_fusion.33
  84.2 1.9 add_select_fusion.10
  86.1 4.8 bitcast_multiply_fusion
  91.0 26.2 %all-reduce.2.cloned.1.call-done = f32[320,256]{1,0:T(8,128)} async-done(((f32[320,256]{1,0:T(8,128)}), f32[320,256]{1,0:T(8,128)}) %all-reduce.2.cloned.1.call-update) | async-done | bytes 327696 | tf_op jit(solution)/shard_map/psum | solution.py:87
  117.2 1.9 broadcast_multiply_fusion
  119.0 608.0 %all-gather.3.cloned.1.call-done = f32[8,256,4096]{2,1,0:T(8,128)} async-done(((f32[1,256,4096]{2,1,0:T(8,128)}), f32[8,256,4096]{2,1,0:T(8,128)}) %all-gather.3.cloned.1.call-update) | async-done | bytes 33554448 | tf_op jit(solution)/shard_map/all_gather | solution.py:81
  727.1 14.0 %reduce_sum.9 = f32[256,4096]{1,0:T(8,128)} reduce(f32[8,256,4096]{2,1,0:T(8,128)} %all-gather.3.cloned.1.call-done, f32[]{:T(128)} %constant.375.clone.1), dimensions={0}, to_apply=%region_1.2 | reduce | flops 7340032 | bytes 37748740 | tf_op jit(solution)/shard_map/reduce_sum | solution.py:82
  741.1 4.5 convolution_remainder_fusion.1
  745.6 2.8 convolution_remainder_fusion.2
  748.4 2.5 convolution_remainder_fusion.3
  751.0 22.2 %fusion.12 = f32[320,4096]{1,0:T(8,128)} fusion(f32[320,4096]{1,0:T(8,128)S(1)} %bitcast.24, f32[320,4096]{1,0:T(8,128)S(1)} %convolution_remainder_fusion.1, f32[320,4096]{1,0:T(8,128)S(1)} %convolution_remainder_fusion.2, f32[320,4096]{1,0:T(8,128)S(1)} %convolution_remainder_fusion.3, f32[256,4096]{1,0:T(8,128)S(1)} %copy-done, f32[320,256]{1,0:T(8,128)S(1)} %copy-done.1), kind=kOutput, calls=%fused_computation.33 | convolution fusion | flops 754565120 | bytes 30736384 | tf_op jit(solution)/shard_map/dot_general | solution.py:35
  (95 shorter events, 26.1 us)
Async XLA Ops:
  8.0 109.2 %all-reduce.2.cloned.1.call-start = ((), (), s32[]{:S(2)}) async-start(), calls=%async_computation | async-start | bytes 655360 | tf_op jit(solution)/shard_map/psum | solution.py:87
  8.7 6.3 collective-permute-start.3
  14.1 15.2 %collective-permute-start = (f32[256,64]{1,0:T(8,128)S(1)}, f32[256,64]{1,0:T(8,128)S(1)}, u32[]{:S(2)}, u32[]{:S(2)}) collective-permute-start(f32[256,64]{1,0:T(8,128)S(1)} %gather_fusion), channel_id=1, source_target_pairs={{0,4},{4,0},{8,12},{12,8},{16,20},{20,16},{24,28},{28,24},{1,5},{5... | collective-permute-start | bytes 196616 | tf_op jit(solution)/shard_map/ppermute | solution.py:16
  17.0 3.7 collective-permute-start.4
  22.7 4.7 collective-permute-start.5
  30.1 5.0 collective-permute-start.1
  35.9 12.0 %collective-permute-start.2 = (f32[256,64]{1,0:T(8,128)S(1)}, f32[256,64]{1,0:T(8,128)S(1)}, u32[]{:S(2)}, u32[]{:S(2)}) collective-permute-start(f32[256,64]{1,0:T(8,128)S(1)} %gather_fusion.2), channel_id=1, source_target_pairs={{0,16},{16,0},{4,20},{20,4},{8,24},{24,8},{12,28},{28,12},{1,17},{... | collective-permute-start | bytes 196616 | tf_op jit(solution)/shard_map/ppermute | solution.py:16
  81.2 2.1 copy-start.2
  86.1 641.0 %all-gather.3.cloned.1.call-start = ((), (), s32[]{:S(2)}) async-start(), calls=%async_computation.1 | async-start | bytes 37748736 | tf_op jit(solution)/shard_map/all_gather | solution.py:81
  119.0 622.0 %copy-start.1 = (f32[320,256]{1,0:T(8,128)S(1)}, f32[320,256]{1,0:T(8,128)}, u32[]{:S(2)}) copy-start(f32[320,256]{1,0:T(8,128)} %all-reduce.2.cloned.1.call-done) | copy-start | bytes 983044
  741.1 4.5 copy-start
  745.6 5.4 slice-start
  748.4 2.6 slice-start.1
Sparse Core Ops, SparseCore 0:
  86.2 30.9 all-reduce.1
Sparse Core Ops, SparseCore 1:
  91.0 636.0 all-gather.2
